TPU v7x, 256 devices: a whole 4x4x8 slice. The times are simulated.
256 devices in a mesh: row: 8 (over x, core), col: 32 (over z, y).
Axes of the slice: x: 4, y: 4, z: 8, core: 2. Of those that a mesh axis runs over, the one named last changes fastest.
Arguments:
- features: float32 [32768, 512], P(('col', 'row')), may hold values from -6 to 6
- weight: float32 [512, 512], replicated, may hold values from -0.25 to 0.25
- cotangent: bfloat16 [32768, 512], P(('row', 'col')), may hold values from -6 to 6
- block_values: bfloat16 [8, 32, 96, 128, 128], P('row', 'col'), may hold values from -0.0625 to 0.0625
- block_coords: int32 [8, 32, 2, 96], P('row', 'col'), may hold values from -1 to 31, as said below
Outputs:
- activated: float32 [32768, 512], P(('row', 'col'))
- dfeatures: float32 [32768, 512], P(('col', 'row'))
- dweight: float32 [512, 512], P('row', 'col')
Inputs may be any that keep to these rules, and one draw needn't show every extreme that they name: block_coords[r, c, 0, s] is a block row below 32 and block_coords[r, c, 1, s] a block column below 8 of slot s of device (r, c), or both are -1 for an unused slot. Used slots come first and name distinct blocks; each device uses between a quarter of 96 (rounded down) and all 96 slots, and some device uses all 96.
All inputs are finite; a program needn't handle non-finite values.
Results may differ from a plain program's by a relative error of at most 0.006.
Values may be sent and summed in bfloat16 or wider, within the bound.
No kernel may reach another device: no remote copies, remote signals or barrier semaphores. Data moves between devices by JAX's collectives and lax.ppermute only.
A program may use at most 128 MiB of HBM per device.

v0:
```python
import jax
import jax.numpy as jnp
from jax import lax
from jax.sharding import PartitionSpec as P


def silu_slope(values):
    sigma = jax.nn.sigmoid(values)
    return sigma * (1.0 + values * (1.0 - sigma))


def group_size():
    return 32


def blocks_forward(slot_values, slot_rows, slot_cols, tile_stack, out_blocks):
    slot_count = slot_values.shape[0]
    group = group_size()
    turn_count = slot_count // group
    block = slot_values.shape[1]
    hidden_width = tile_stack.shape[-1]

    def add_group(totals, slot_item):
        group_vals, row_ids, col_ids = slot_item
        selected = jnp.take(tile_stack, col_ids, axis=0)
        products = jnp.einsum(
            "sab,sbc->sac", group_vals, selected, preferred_element_type=jnp.float32
        )
        return (totals.at[row_ids].add(products), None)

    zero_sums = jnp.zeros((out_blocks, block, hidden_width), jnp.float32)
    totals, _ = lax.scan(
        add_group,
        zero_sums,
        (
            slot_values.reshape(turn_count, group, block, block),
            slot_rows.reshape(turn_count, group),
            slot_cols.reshape(turn_count, group),
        ),
    )
    return totals.reshape(out_blocks * block, hidden_width)


def blocks_backward(slot_values, slot_rows, slot_cols, tile_stack, out_blocks):
    slot_count = slot_values.shape[0]
    group = group_size()
    turn_count = slot_count // group
    block = slot_values.shape[1]
    hidden_width = tile_stack.shape[-1]

    def add_group(totals, slot_item):
        group_vals, row_ids, col_ids = slot_item
        selected = jnp.take(tile_stack, row_ids, axis=0)
        products = jnp.einsum(
            "sab,sac->sbc", group_vals, selected, preferred_element_type=jnp.float32
        )
        return (totals.at[col_ids].add(products), None)

    zero_sums = jnp.zeros((out_blocks, block, hidden_width), jnp.float32)
    totals, _ = lax.scan(
        add_group,
        zero_sums,
        (
            slot_values.reshape(turn_count, group, block, block),
            slot_rows.reshape(turn_count, group),
            slot_cols.reshape(turn_count, group),
        ),
    )
    return totals.reshape(out_blocks * block, hidden_width)


def on_device(features, weight, cotangent, block_values, block_coords):
    slot_values = block_values[0, 0]
    coordinate = block_coords[0, 0]
    live_slots = coordinate[0] >= 0
    slot_values = jnp.where(live_slots[:, None, None], slot_values, jnp.zeros_like(slot_values))
    slot_rows = jnp.maximum(coordinate[0], 0)
    slot_cols = jnp.maximum(coordinate[1], 0)
    block = slot_values.shape[1]
    own_rows = features.shape[0]
    hidden_width = features.shape[1]
    col_count = lax.axis_size("col")
    row_count = lax.axis_size("row")
    row_blocks = col_count * own_rows // block
    col_blocks = row_count * own_rows // block
    gathered_cot = lax.all_gather(cotangent, "col", axis=0, tiled=True)
    xcopy = features.astype(jnp.bfloat16)
    wcopy = weight.astype(jnp.bfloat16)
    projected = jnp.dot(xcopy, wcopy, preferred_element_type=jnp.float32).astype(jnp.bfloat16)
    column_rows = lax.all_gather(projected, "row", axis=0, tiled=True)
    partial_value = blocks_forward(
        slot_values,
        slot_rows,
        slot_cols,
        column_rows.reshape(col_blocks, block, hidden_width),
        row_blocks,
    )
    full_sums = lax.psum(partial_value, "col")
    row_start = lax.axis_index("col") * own_rows
    own_sums = lax.dynamic_slice_in_dim(full_sums, row_start, own_rows, 0)
    activated = jax.nn.silu(own_sums)
    slope_rows = (gathered_cot.astype(jnp.float32) * silu_slope(full_sums)).astype(jnp.bfloat16)
    column_part = blocks_backward(
        slot_values,
        slot_rows,
        slot_cols,
        slope_rows.reshape(row_blocks, block, hidden_width),
        col_blocks,
    )
    node_grad = lax.psum_scatter(column_part, "row", scatter_dimension=0, tiled=True)
    grad_copy = node_grad.astype(jnp.bfloat16)
    dfeatures = jnp.dot(grad_copy, wcopy.T, preferred_element_type=jnp.float32)
    local_weight = jnp.dot(xcopy.T, grad_copy, preferred_element_type=jnp.float32)
    weight_part = lax.psum_scatter(local_weight, "row", scatter_dimension=0, tiled=True)
    node_total = own_rows * row_count * col_count
    dweight = lax.psum_scatter(weight_part, "col", scatter_dimension=1, tiled=True) * (
        1.0 / node_total**0.5
    )
    return (activated, dfeatures, dweight)


def solution(mesh):
    placed = (
        P(("col", "row"), None),
        P(),
        P(("row", "col"), None),
        P("row", "col", None, None, None),
        P("row", "col", None, None),
    )
    return jax.shard_map(
        on_device,
        mesh=mesh,
        in_specs=placed,
        out_specs=(P(("row", "col"), None), P(("col", "row"), None), P("row", "col")),
        check_vma=False,
    )
```

profile of v0, /device:TPU:2, one launch (start us, length us, event | category | flops | bytes accessed | tf_op | source)
XLA Modules:
  0.0 720.8 jit_solution(8900149121695483579)
XLA Ops:
  7.2 2.2 convolution_convert_fusion
  11.1 3.5 copy.10
  14.8 2.0 broadcast_select_fusion
  16.8 20.7 %all-gather.3.cloned.1.call-done = bf16[1024,512]{1,0:T(8,128)(2,1)} async-done(((bf16[128,512]{1,0:T(8,128)(2,1)}), bf16[1024,512]{1,0:T(8,128)(2,1)}) %all-gather.3.cloned.1.call-update) | async-done | bytes 1048592 | tf_op jit(solution)/shard_map/all_gather | solution.py:90
  37.6 4.3 broadcast_in_dim.40
  41.9 86.4 %while.20 = (s32[]{:T(128)}, f32[32,128,512]{2,1,0:T(8,128)}, s32[3,32]{1,0:T(4,128)S(1)}, bf16[3,32,128,128]{2,3,1,0:T(8,128)(2,1)}, s32[3,32]{1,0:T(4,128)S(1)}, /*index=5*/bf16[8,128,512]{2,1,0:T(8,128)(2,1)S(1)}, s32[]{:T(128)}) while((s32[]{:T(128)}, f32[32,128,512]{2,1,0:T(8,128)}, s32[3,32]{1,0:T(4,128)S(1)}, ...), condition=%wide.region_2.3_spmd, body=%wide.region_0.2_spmd.sunk | while | flops 541066624 | bytes 47191200 | solution.py:32
  41.9 2.8 gather_fusion
  44.7 7.1 fusion.40
  51.8 18.9 %scatter_fusion = f32[32,128,512]{2,1,0:T(8,128)} fusion(f32[32,128,512]{2,1,0:T(8,128)} %get-tuple-element.201, s32[32]{0:T(128)S(1)} %get-tuple-element.183, f32[32,128,512]{2,1,0:T(8,128)} %fusion.40), kind=kCustom, calls=%fused_computation.2.clone.1 | custom fusion | flops 2097152 | bytes 25165952 | tf_op jit(solution)/shard_map/while/body/eval_jaxpr/scatter-add | solution.py:29
  70.7 2.8 gather_fusion
  73.5 7.1 fusion.40
  80.6 19.0 %scatter_fusion = f32[32,128,512]{2,1,0:T(8,128)} fusion(f32[32,128,512]{2,1,0:T(8,128)} %get-tuple-element.201, s32[32]{0:T(128)S(1)} %get-tuple-element.183, f32[32,128,512]{2,1,0:T(8,128)} %fusion.40), kind=kCustom, calls=%fused_computation.2.clone.1 | custom fusion | flops 2097152 | bytes 25165952 | tf_op jit(solution)/shard_map/while/body/eval_jaxpr/scatter-add | solution.py:29
  99.6 2.8 gather_fusion
  102.4 7.1 fusion.40
  109.5 18.8 %scatter_fusion = f32[32,128,512]{2,1,0:T(8,128)} fusion(f32[32,128,512]{2,1,0:T(8,128)} %get-tuple-element.201, s32[32]{0:T(128)S(1)} %get-tuple-element.183, f32[32,128,512]{2,1,0:T(8,128)} %fusion.40), kind=kCustom, calls=%fused_computation.2.clone.1 | custom fusion | flops 2097152 | bytes 25165952 | tf_op jit(solution)/shard_map/while/body/eval_jaxpr/scatter-add | solution.py:29
  128.4 213.3 %all-reduce.2.cloned.1.call-done = f32[4096,512]{1,0:T(8,128)} async-done(((f32[4096,512]{1,0:T(8,128)}), f32[4096,512]{1,0:T(8,128)}) %all-reduce.2.cloned.1.call-update) | async-done | bytes 8388624 | tf_op jit(solution)/shard_map/psum | solution.py:98
  341.7 7.6 %multiply_convert_fusion = bf16[4096,512]{1,0:T(8,128)(2,1)} fusion(f32[4096,512]{1,0:T(8,128)} %all-reduce.2.cloned.1.call-done, bf16[4096,512]{1,0:T(8,128)(2,1)} %all-gather.5.cloned.1.call-done), kind=kLoop, calls=%fused_computation.40 | loop fusion | flops 20971520 | bytes 16777216 | tf_op jit(solution)/shard_map/convert_element_type | solution.py:102
  349.6 71.1 %while.21 = (s32[]{:T(128)}, f32[8,128,512]{2,1,0:T(8,128)S(1)}, s32[3,32]{1,0:T(4,128)S(1)}, bf16[3,32,128,128]{2,3,1,0:T(8,128)(2,1)}, s32[3,32]{1,0:T(4,128)S(1)}, /*index=5*/bf16[32,128,512]{2,1,0:T(8,128)(2,1)}, s32[]{:T(128)}) while((s32[]{:T(128)}, f32[8,128,512]{2,1,0:T(8,128)S(1)}, s32[3,32]{1,0:T(4,128)S(1)}, ...), condition=%wide.region_6.7_spmd, body=%wide.region_4.6_spmd.sunk | while | flops 541066624 | bytes 47191200 | solution.py:60
  349.6 5.0 gather_fusion.1
  354.6 7.1 fusion.44
  361.7 11.8 %scatter_fusion.1 = f32[8,128,512]{2,1,0:T(8,128)S(1)} fusion(f32[8,128,512]{2,1,0:T(8,128)S(1)} %get-tuple-element.222, s32[32]{0:T(128)S(1)} %get-tuple-element.191, f32[32,128,512]{2,1,0:T(8,128)} %fusion.44), kind=kCustom, calls=%fused_computation.3.clone.1 | custom fusion | flops 2097152 | bytes 25165952 | tf_op jit(solution)/shard_map/while/body/eval_jaxpr/scatter-add | solution.py:57
  373.5 4.9 gather_fusion.1
  378.4 7.1 fusion.44
  385.5 11.6 %scatter_fusion.1 = f32[8,128,512]{2,1,0:T(8,128)S(1)} fusion(f32[8,128,512]{2,1,0:T(8,128)S(1)} %get-tuple-element.222, s32[32]{0:T(128)S(1)} %get-tuple-element.191, f32[32,128,512]{2,1,0:T(8,128)} %fusion.44), kind=kCustom, calls=%fused_computation.3.clone.1 | custom fusion | flops 2097152 | bytes 25165952 | tf_op jit(solution)/shard_map/while/body/eval_jaxpr/scatter-add | solution.py:57
  397.2 4.9 gather_fusion.1
  402.1 7.1 fusion.44
  409.2 11.5 %scatter_fusion.1 = f32[8,128,512]{2,1,0:T(8,128)S(1)} fusion(f32[8,128,512]{2,1,0:T(8,128)S(1)} %get-tuple-element.222, s32[32]{0:T(128)S(1)} %get-tuple-element.191, f32[32,128,512]{2,1,0:T(8,128)} %fusion.44), kind=kCustom, calls=%fused_computation.3.clone.1 | custom fusion | flops 2097152 | bytes 25165952 | tf_op jit(solution)/shard_map/while/body/eval_jaxpr/scatter-add | solution.py:57
  422.1 32.0 %reduce-scatter.6.cloned.1.call-done = f32[128,512]{1,0:T(8,128)} async-done(((f32[1024,512]{1,0:T(8,128)}), f32[128,512]{1,0:T(8,128)}) %reduce-scatter.6.cloned.1.call-update) | async-done | bytes 262160 | tf_op jit(solution)/shard_map/reduce_scatter | solution.py:110
  457.0 1.7 divide_multiply_fusion
  458.7 32.1 %reduce-scatter.10.cloned.1.call-done = f32[64,512]{1,0:T(8,128)} async-done(((f32[512,512]{1,0:T(8,128)}), f32[64,512]{1,0:T(8,128)}) %reduce-scatter.10.cloned.1.call-update) | async-done | bytes 131088
  490.8 1.7 copy.13
  493.6 219.0 %reduce-scatter.8.cloned.1.call-done = f32[64,16]{0,1:T(8,128)} async-done(((f32[64,512]{0,1:T(8,128)}), f32[64,16]{0,1:T(8,128)}) %reduce-scatter.8.cloned.1.call-update) | async-done | bytes 4112 | tf_op jit(solution)/shard_map/reduce_scatter | solution.py:116
  (53 shorter events, 8.9 us)
Async XLA Ops:
  7.2 7.4 %copy-start.5 = (s32[1,1,2,96]{3,2,1,0:T(2,128)S(1)}, s32[1,1,2,96]{3,2,1,0:T(2,128)}, u32[]{:S(2)}) copy-start(s32[1,1,2,96]{3,2,1,0:T(2,128)} %param.13) | copy-start | bytes 2308
  7.2 30.4 %all-gather.3.cloned.1.call-start = ((), (), s32[]{:S(2)}) async-start(), calls=%async_computation.3 | async-start | bytes 1179648 | tf_op jit(solution)/shard_map/all_gather | solution.py:90
  9.5 118.9 %all-gather.5.cloned.1.call-start = ((), (), s32[]{:S(2)}) async-start(), calls=%async_computation.5 | async-start | bytes 4325376 | tf_op jit(solution)/shard_map/all_gather | solution.py:86
  10.2 331.5 %all-reduce.2.cloned.1.call-start = ((), (), s32[]{:S(2)}) async-start(), calls=%async_computation.4 | async-start | bytes 16777216 | tf_op jit(solution)/shard_map/psum | solution.py:98
  37.6 4.3 copy-start.1
  128.3 325.9 %reduce-scatter.6.cloned.1.call-start = ((), (), s32[]{:S(2)}) async-start(), calls=%async_computation.6 | async-start | bytes 2359296 | tf_op jit(solution)/shard_map/reduce_scatter | solution.py:110
  349.6 104.6 %copy-start.3 = (f32[128,512]{1,0:T(8,128)S(1)}, f32[128,512]{1,0:T(8,128)}, u32[]{:S(2)}) copy-start(f32[128,512]{1,0:T(8,128)} %param.9) | copy-start | bytes 786436
  420.7 1.4 copy-start
  420.7 71.9 %copy-start.2 = (f32[512,512]{1,0:T(8,128)S(1)}, f32[512,512]{1,0:T(8,128)}, u32[]{:S(2)}) copy-start(f32[512,512]{1,0:T(8,128)} %param.10) | copy-start | bytes 3145732
  422.1 68.7 %reduce-scatter.10.cloned.1.call-start = ((), (), s32[]{:S(2)}) async-start(), calls=%async_computation.8 | async-start | bytes 1179648
  454.2 38.4 %copy-start.4 = (f32[128,512]{1,0:T(8,128)S(1)}, f32[128,512]{1,0:T(8,128)}, u32[]{:S(2)}) copy-start(f32[128,512]{1,0:T(8,128)} %reduce-scatter.6.cloned.1.call-done) | copy-start | bytes 786436
  456.9 255.7 %reduce-scatter.8.cloned.1.call-start = ((), (), s32[]{:S(2)}) async-start(), calls=%async_computation.7 | async-start | bytes 270336 | tf_op jit(solution)/shard_map/reduce_scatter | solution.py:116
Sparse Core Ops, SparseCore 0:
  10.4 27.1 all-gather.2
  40.2 83.2 all-gather.4
  128.4 213.2 all-reduce.1
  422.2 31.9 reduce-scatter.5
  457.1 33.7 reduce-scatter.9
  494.5 218.0 reduce-scatter.7
where the time goes:
time: 722 us; the launch traced here: 721 us
  waiting for transfers between devices  518 us (72%)
  other arithmetic  105 us (15%)
  matrix products  47 us (7%)
  local copies, waits for them, and re-layouts  36 us (5%)
  between operations  14.2 us (2%)
    reduce_scatter x1, waiting for transfers between devices, on_device(): lax.psum_scatter(weight_part, 'col', scatter_dimension=1, tiled=True)  219 us
    psum x1, waiting for transfers between devices, on_device(): full_sums = lax.psum(partial_value, 'col')  213 us
    scatter-add x3, other arithmetic, add_group(): return (totals.at[row_ids].add(products), None)  56.7 us
    scatter-add x3, other arithmetic, add_group(): return (totals.at[col_ids].add(products), None)  34.9 us
    unnamed x7, waiting for transfers between devices  32.9 us
    reduce_scatter x1, waiting for transfers between devices, on_device(): lax.psum_scatter(column_part, 'row', scatter_dimension=0, tiled=True)  32 us
    dot_general x3, matrix products, add_group(): jnp.einsum('sab,sbc->sac', group_vals, selected, preferred_element_type=j...  21.3 us
    dot_general x3, matrix products, add_group(): jnp.einsum('sab,sac->sbc', group_vals, selected, preferred_element_type=j...  21.2 us
  transfers between devices with their start and end apart: 6, of which 5 were waited for; matrix products, arithmetic and copies ran while one was open for 14% of the time, Pallas kernels for 0%

commit v1 on v0

--- a/solution.py
+++ b/solution.py
@@ -2,6 +2,15 @@
 import jax.numpy as jnp
 from jax import lax
 from jax.sharding import PartitionSpec as P
+
+
+def sum_by_hops(block, name):
+    n_dev = lax.axis_size(name)
+    total, far = (block, 1)
+    while far < n_dev:
+        total = total + lax.ppermute(total, name, [(i, i ^ far) for i in range(n_dev)])
+        far = 2 * far
+    return total
 
 
 def silu_slope(values):
@@ -95,7 +104,7 @@
         column_rows.reshape(col_blocks, block, hidden_width),
         row_blocks,
     )
-    full_sums = lax.psum(partial_value, "col")
+    full_sums = sum_by_hops(partial_value, "col")
     row_start = lax.axis_index("col") * own_rows
     own_sums = lax.dynamic_slice_in_dim(full_sums, row_start, own_rows, 0)
     activated = jax.nn.silu(own_sums)

time: 722 us -> 1880 us (2.60)
  waiting for transfers between devices: 518 us -> 1610 us
  other arithmetic: 105 us -> 153 us
    ppermute x0 -> x5, waiting for transfers between devices: none -> 903 us  [sum_by_hops(): lax.ppermute(total, name, [(i, i ^ far) for i in range(n_dev)])]
    all_gather x1, waiting for transfers between devices: 0.02 us -> 409 us  [on_device(): gathered_cot = lax.all_gather(cotangent, 'col', axis=0, tiled=True)]
    psum x1 -> x0, waiting for transfers between devices: 213 us -> none  [on_device(): full_sums = lax.psum(partial_value, 'col')]
    add x0 -> x4, other arithmetic: none -> 44.4 us  [sum_by_hops(): total + lax.ppermute(total, name, [(i, i ^ far) for i in range(n_dev)])]
  transfers between devices with their start and end apart: 6 -> 10, of which waited for: 5 -> 9; matrix products, arithmetic and copies ran while one was open for 14% -> 1% of each run, Pallas kernels for 0% -> 0%
where the time goes in v1:
time: 1880 us
  waiting for transfers between devices  1610 us (86%)
  other arithmetic  153 us (8%)
  matrix products  47.8 us (3%)
  local copies, waits for them, and re-layouts  36 us (2%)
    ppermute x5, waiting for transfers between devices, sum_by_hops(): lax.ppermute(total, name, [(i, i ^ far) for i in range(n_dev)])  903 us
    all_gather x1, waiting for transfers between devices, on_device(): gathered_cot = lax.all_gather(cotangent, 'col', axis=0, tiled=True)  409 us
    reduce_scatter x1, waiting for transfers between devices, on_device(): lax.psum_scatter(weight_part, 'col', scatter_dimension=1, tiled=True)  216 us
    scatter-add x3, other arithmetic, add_group(): return (totals.at[row_ids].add(products), None)  54.8 us
    add x4, other arithmetic, sum_by_hops(): total + lax.ppermute(total, name, [(i, i ^ far) for i in range(n_dev)])  44.4 us
  transfers between devices with their start and end apart: 10, of which 9 were waited for; matrix products, arithmetic and copies ran while one was open for 1% of the time, Pallas kernels for 0%

profile of v1, /device:TPU:2, one launch (start us, length us, event | category | flops | bytes accessed | tf_op | source)
XLA Modules:
  0.0 1876.6 jit_solution(15793965232410773126)
XLA Ops:
  17.6 20.8 %all-gather.3.cloned.1.call-done = bf16[1024,512]{1,0:T(8,128)(2,1)} async-done(((bf16[128,512]{1,0:T(8,128)(2,1)}), bf16[1024,512]{1,0:T(8,128)(2,1)}) %all-gather.3.cloned.1.call-update) | async-done | bytes 1048592 | tf_op jit(solution)/shard_map/all_gather | solution.py:99
  38.4 4.3 broadcast_in_dim.40
  42.7 84.4 %while.20 = (s32[]{:T(128)}, f32[32,128,512]{2,1,0:T(8,128)}, s32[3,32]{1,0:T(4,128)S(1)}, bf16[3,32,128,128]{2,3,1,0:T(8,128)(2,1)}, s32[3,32]{1,0:T(4,128)S(1)}, /*index=5*/bf16[8,128,512]{2,1,0:T(8,128)(2,1)S(1)}, s32[]{:T(128)}) while((s32[]{:T(128)}, f32[32,128,512]{2,1,0:T(8,128)}, s32[3,32]{1,0:T(4,128)S(1)}, ...), condition=%wide.region_2.3_spmd, body=%wide.region_0.2_spmd.sunk | while | flops 541066624 | bytes 47191700 | solution.py:41
  45.5 7.1 fusion.40
  52.6 18.6 scatter_fusion
  74.0 7.1 fusion.40
  81.0 18.3 scatter_fusion
  102.2 7.1 fusion.40
  109.3 17.9 scatter_fusion
  129.9 181.0 %collective-permute-done = f32[4096,512]{1,0:T(8,128)} collective-permute-done((f32[4096,512]{1,0:T(8,128)}, f32[4096,512]{1,0:T(8,128)}, u32[]{:S(2)}, u32[]{:S(2)}) %collective-permute-start) | collective-permute-done | bytes 8388640 | tf_op jit(solution)/shard_map/ppermute | solution.py:11
  310.9 11.1 bitcast_add_fusion
  324.3 181.4 %collective-permute-done.1 = f32[4096,512]{1,0:T(8,128)} collective-permute-done((f32[4096,512]{1,0:T(8,128)}, f32[4096,512]{1,0:T(8,128)}, u32[]{:S(2)}, u32[]{:S(2)}) %collective-permute-start.1) | collective-permute-done | bytes 8388640 | tf_op jit(solution)/shard_map/ppermute | solution.py:11
  505.7 11.1 add.107
  517.3 180.8 %collective-permute-done.2 = f32[4096,512]{1,0:T(8,128)} collective-permute-done((f32[4096,512]{1,0:T(8,128)}, f32[4096,512]{1,0:T(8,128)}, u32[]{:S(2)}, u32[]{:S(2)}) %collective-permute-start.2) | collective-permute-done | bytes 8388640 | tf_op jit(solution)/shard_map/ppermute | solution.py:11
  698.1 11.1 add.108
  712.9 359.4 %collective-permute-done.3 = f32[4096,512]{1,0:T(8,128)} collective-permute-done((f32[4096,512]{1,0:T(8,128)}, f32[4096,512]{1,0:T(8,128)}, u32[]{:S(2)}, u32[]{:S(2)}) %collective-permute-start.3) | collective-permute-done | bytes 8388640 | tf_op jit(solution)/shard_map/ppermute | solution.py:11
  1072.3 11.1 add.109
  1087.6 409.1 %all-gather.5.cloned.1.call-done = bf16[4096,512]{1,0:T(8,128)(2,1)} async-done(((bf16[128,512]{1,0:T(8,128)(2,1)}), bf16[4096,512]{1,0:T(8,128)(2,1)}) %all-gather.5.cloned.1.call-update) | async-done | bytes 4194320 | tf_op jit(solution)/shard_map/all_gather | solution.py:95
  1496.7 12.0 multiply_convert_fusion
  1509.0 71.2 %while.21 = (s32[]{:T(128)}, f32[8,128,512]{2,1,0:T(8,128)S(1)}, s32[3,32]{1,0:T(4,128)S(1)}, bf16[3,32,128,128]{2,3,1,0:T(8,128)(2,1)}, s32[3,32]{1,0:T(4,128)S(1)}, /*index=5*/bf16[32,128,512]{2,1,0:T(8,128)(2,1)}, s32[]{:T(128)}) while((s32[]{:T(128)}, f32[8,128,512]{2,1,0:T(8,128)S(1)}, s32[3,32]{1,0:T(4,128)S(1)}, ...), condition=%wide.region_5.6_spmd, body=%wide.region_3.5_spmd.sunk | while | flops 541066624 | bytes 47191700 | solution.py:69
  1509.0 5.0 gather_fusion.1
  1514.1 7.1 fusion.44
  1521.1 11.8 scatter_fusion.1
  1532.9 5.0 gather_fusion.1
  1537.9 7.1 fusion.44
  1545.0 11.6 scatter_fusion.1
  1556.7 5.0 gather_fusion.1
  1561.6 7.1 fusion.44
  1568.7 11.5 scatter_fusion.1
  1581.7 30.0 %reduce-scatter.6.cloned.1.call-done = f32[128,512]{1,0:T(8,128)} async-done(((f32[1024,512]{1,0:T(8,128)}), f32[128,512]{1,0:T(8,128)}) %reduce-scatter.6.cloned.1.call-update) | async-done | bytes 262160 | tf_op jit(solution)/shard_map/reduce_scatter | solution.py:119
  1616.1 32.2 %reduce-scatter.10.cloned.1.call-done = f32[64,512]{1,0:T(8,128)} async-done(((f32[512,512]{1,0:T(8,128)}), f32[64,512]{1,0:T(8,128)}) %reduce-scatter.10.cloned.1.call-update) | async-done | bytes 131088
  1652.0 216.1 %reduce-scatter.8.cloned.1.call-done = f32[64,16]{0,1:T(8,128)} async-done(((f32[64,512]{0,1:T(8,128)}), f32[64,16]{0,1:T(8,128)}) %reduce-scatter.8.cloned.1.call-update) | async-done | bytes 4112 | tf_op jit(solution)/shard_map/reduce_scatter | solution.py:125
  (60 shorter events, 42.5 us)
Async XLA Ops:
  8.0 30.4 %all-gather.3.cloned.1.call-start = ((), (), s32[]{:S(2)}) async-start(), calls=%async_computation.3 | async-start | bytes 1179648 | tf_op jit(solution)/shard_map/all_gather | solution.py:99
  10.3 1486.4 %all-gather.5.cloned.1.call-start = ((), (), s32[]{:S(2)}) async-start(), calls=%async_computation.4 | async-start | bytes 4325376 | tf_op jit(solution)/shard_map/all_gather | solution.py:95
  38.4 4.3 copy-start.1
  127.1 183.8 %collective-permute-start = (f32[4096,512]{1,0:T(8,128)}, f32[4096,512]{1,0:T(8,128)}, u32[]{:S(2)}, u32[]{:S(2)}) collective-permute-start(f32[4096,512]{1,0:T(8,128)} %bitcast.62), channel_id=1, source_target_pairs={{0,1},{1,0},{2,3},{3,2},{4,5},{5,4},{6,7},{7,6},{8,9},{9,8},{10,11... | collective-permute-start | bytes 25165832 | tf_op jit(solution)/shard_map/ppermute | solution.py:11
  322.0 183.7 %collective-permute-start.1 = (f32[4096,512]{1,0:T(8,128)}, f32[4096,512]{1,0:T(8,128)}, u32[]{:S(2)}, u32[]{:S(2)}) collective-permute-start(f32[4096,512]{1,0:T(8,128)} %bitcast_add_fusion), channel_id=1, source_target_pairs={{0,2},{1,3},{2,0},{3,1},{4,6},{5,7},{6,4},{7,5},{8,10},{9,11},{10,... | collective-permute-start | bytes 25165832 | tf_op jit(solution)/shard_map/ppermute | solution.py:11
  516.8 181.4 %collective-permute-start.2 = (f32[4096,512]{1,0:T(8,128)}, f32[4096,512]{1,0:T(8,128)}, u32[]{:S(2)}, u32[]{:S(2)}) collective-permute-start(f32[4096,512]{1,0:T(8,128)} %add.107), channel_id=1, source_target_pairs={{0,4},{1,5},{2,6},{3,7},{4,0},{5,1},{6,2},{7,3},{8,12},{9,13},{10,... | collective-permute-start | bytes 25165832 | tf_op jit(solution)/shard_map/ppermute | solution.py:11
  709.2 363.0 %collective-permute-start.3 = (f32[4096,512]{1,0:T(8,128)}, f32[4096,512]{1,0:T(8,128)}, u32[]{:S(2)}, u32[]{:S(2)}) collective-permute-start(f32[4096,512]{1,0:T(8,128)} %add.108), channel_id=1, source_target_pairs={{0,8},{1,9},{2,10},{3,11},{4,12},{5,13},{6,14},{7,15},{8,0},{9,1},... | collective-permute-start | bytes 25165832 | tf_op jit(solution)/shard_map/ppermute | solution.py:11
  1083.4 413.3 %collective-permute-start.4 = (f32[4096,512]{1,0:T(8,128)}, f32[4096,512]{1,0:T(8,128)}, u32[]{:S(2)}, u32[]{:S(2)}) collective-permute-start(f32[4096,512]{1,0:T(8,128)} %add.109), channel_id=1, source_target_pairs={{0,16},{1,17},{2,18},{3,19},{4,20},{5,21},{6,22},{7,23},{8,24},{9,... | collective-permute-start | bytes 25165832 | tf_op jit(solution)/shard_map/ppermute | solution.py:11
  1087.5 524.2 %reduce-scatter.6.cloned.1.call-start = ((), (), s32[]{:S(2)}) async-start(), calls=%async_computation.5 | async-start | bytes 2359296 | tf_op jit(solution)/shard_map/reduce_scatter | solution.py:119
  1509.0 102.7 %copy-start.3 = (f32[128,512]{1,0:T(8,128)S(1)}, f32[128,512]{1,0:T(8,128)}, u32[]{:S(2)}) copy-start(f32[128,512]{1,0:T(8,128)} %param.9) | copy-start | bytes 786436
  1580.2 1.4 copy-start
  1580.3 69.8 %copy-start.2 = (f32[512,512]{1,0:T(8,128)S(1)}, f32[512,512]{1,0:T(8,128)}, u32[]{:S(2)}) copy-start(f32[512,512]{1,0:T(8,128)} %param.10) | copy-start | bytes 3145732
  1581.6 66.7 %reduce-scatter.10.cloned.1.call-start = ((), (), s32[]{:S(2)}) async-start(), calls=%async_computation.7 | async-start | bytes 1179648
  1614.3 253.9 %reduce-scatter.8.cloned.1.call-start = ((), (), s32[]{:S(2)}) async-start(), calls=%async_computation.6 | async-start | bytes 270336 | tf_op jit(solution)/shard_map/reduce_scatter | solution.py:125
Sparse Core Ops, SparseCore 0:
  11.2 27.1 all-gather.2
  1581.7 29.9 reduce-scatter.5
  1614.4 33.8 reduce-scatter.9
Sparse Core Ops, SparseCore 1:
  1087.6 409.0 all-gather.4
  1650.1 218.0 reduce-scatter.7
